TPU v7x, 256 devices: a whole 4x4x8 slice. The times are simulated.
256 devices in a mesh: row: 8 (over z_lo, y), col: 32 (over x, z_hi, core).
Axes of the slice: x: 4, y: 4, z: 8 (z_hi: 4, z_lo: 2; z = z_hi * 2 + z_lo), core: 2. Of those that a mesh axis runs over, the one named last changes fastest.
Arguments:
- feature_map: bfloat16 [1024, 1024, 64], P('row', 'col'), may hold values from -6 to 6
- first_conv_weight: bfloat16 [3, 3, 64, 64], replicated, may hold values from -0.25 to 0.25
- first_conv_bias: float32 [64], replicated, may hold values from -3 to 3
- second_conv_weight: bfloat16 [3, 3, 64, 64], replicated, may hold values from -0.25 to 0.25
- second_conv_bias: float32 [64], replicated, may hold values from -3 to 3
- cotangent: bfloat16 [1024, 1024, 64], P('row', 'col'), may hold values from -6 to 6
Outputs:
- output: bfloat16 [1024, 1024, 64], P('row', 'col')
- grad_input: bfloat16 [1024, 1024, 64], P('row', 'col')
All inputs are finite; a program needn't handle non-finite values.
Results may differ from a plain program's by a relative error of at most 0.0058.
Values may be sent and summed in bfloat16 or wider, within the bound.
A program may use at most 64 MiB of HBM per device.

v0:
```python
import functools

import jax
import jax.numpy as jnp
from jax import lax
from jax.experimental import pallas as pl
from jax.experimental.pallas import tpu as pltpu
from jax.sharding import PartitionSpec as P

MESH = pl.DeviceIdType.MESH
STEP = 4
PHASES = STEP * STEP
F32 = jnp.float32
BF16 = jnp.bfloat16
ROOT_HALF = 0.7071067811865476
INV_ROOT_TAU = 0.3989422804014327
DIRECTIONS = [(-1, 0), (1, 0), (0, -1), (0, 1), (-1, -1), (-1, 1), (1, -1), (1, 1)]
NT = (((1,), (1,)), ((), ()))
TN = (((0,), (0,)), ((), ()))


def iota2(shape, dim):
    return lax.broadcasted_iota(jnp.int32, shape, dim)


def dot(a, b, dims=None):
    if dims is None:
        return jnp.dot(a, b, preferred_element_type=F32)
    return lax.dot_general(a, b, dims, preferred_element_type=F32)


def gelu_and_slope(v):
    half_cdf = 0.5 * (1.0 + lax.erf(v * ROOT_HALF))
    return v * half_cdf, half_cdf + v * jnp.exp(-0.5 * v * v) * INV_ROOT_TAU


def gelu_value(v):
    return 0.5 * v * (1.0 + lax.erf(v * ROOT_HALF))


def kernel(
    rows_axis,
    cols_axis,
    feature,
    w_first,
    b_first,
    w_second,
    b_second,
    cotangent,
    out_ref,
    grad_ref,
    entry,
    own,
    cot,
    sym,
    hid,
    g2,
    g1,
    gsym,
    fresh,
    slope,
    packed,
    inbox1,
    inbox2,
    halo_send,
    halo_recv,
    turn_send,
    turn_recv,
):
    C = w_first.shape[-1]
    TC, _, TR = feature.shape
    nI, nP = TR // STEP, TC // (2 * STEP)
    QB = TC // STEP
    NQ = TR // TC
    L = 2 * C
    r, c = lax.axis_index("row"), lax.axis_index("col")

    def partner(q):
        return (c // NQ, r * NQ + q)

    def is_self(q):
        return jnp.logical_and(c // NQ == r, r * NQ + q == c)

    def exists(d):
        dr, dc = d
        ok = None
        for delta, pos, size in ((dr, r, rows_axis), (dc, c, cols_axis)):
            if delta == -1:
                cond = pos > 0
            elif delta == 1:
                cond = pos < size - 1
            else:
                continue
            ok = cond if ok is None else jnp.logical_and(ok, cond)
        return ok

    for img in (sym, g2):
        img[0:2] = jnp.zeros((2, nP + 2, PHASES, L), BF16)
        img[nI + 2 : nI + 4] = jnp.zeros((2, nP + 2, PHASES, L), BF16)
        img[:, 0:1] = jnp.zeros((nI + 4, 1, PHASES, L), BF16)
        img[:, nP + 1 : nP + 2] = jnp.zeros((nI + 4, 1, PHASES, L), BF16)

    barrier = pltpu.get_barrier_semaphore()
    expected = jnp.int32(0)
    for q in range(NQ):
        other = jnp.logical_not(is_self(q))
        expected = expected + other.astype(jnp.int32)

        @pl.when(other)
        def _():
            pl.semaphore_signal(barrier, inc=1, device_id=partner(q), device_id_type=MESH)

    for d in DIRECTIONS:
        here = exists(d)
        expected = expected + here.astype(jnp.int32)

        @pl.when(here)
        def _():
            pl.semaphore_signal(
                barrier, inc=1, device_id=(r + d[0], c + d[1]), device_id_type=MESH
            )

    shape = (nI * PHASES, STEP * TR)
    at = iota2(shape, 0)
    target = ((at // STEP) % STEP) * TR + (at // PHASES) * STEP + at % STEP
    entry[...] = jnp.where(iota2(shape, 1) == target, 1.0, 0.0).astype(BF16)

    def enter(src, dst):
        for jp in range(nP):
            base = jp * 2 * STEP
            blocks = [
                jnp.concatenate([src[base + s], src[base + STEP + s]], axis=0) for s in range(STEP)
            ]
            res = dot(entry[...], jnp.concatenate(blocks, axis=1), NT)
            dst[:, jp] = res.astype(BF16).reshape(nI, PHASES, L)

    def leave(src, dst):
        for jp in range(nP):
            base = jp * 2 * STEP
            res = dot(src[:, jp].reshape(nI * PHASES, L), entry[...], TN).astype(BF16)
            for b in range(2):
                for s in range(STEP):
                    dst[base + STEP * b + s] = res[b * C : (b + 1) * C, s * TR : (s + 1) * TR]

    def turn_copy(src, inbox, k, q):
        return pltpu.make_async_remote_copy(
            src_ref=src.at[pl.ds(q * QB, QB)],
            dst_ref=inbox.at[lax.rem(c, NQ)],
            send_sem=turn_send.at[k, q],
            recv_sem=turn_recv.at[k, lax.rem(c, NQ)],
            device_id=partner(q),
            device_id_type=MESH,
        )

    def turn_start(src, inbox, k, q):
        mine = is_self(q)

        @pl.when(jnp.logical_not(mine))
        def _():
            turn_copy(src, inbox, k, q).start()

        @pl.when(mine)
        def _():
            pltpu.make_async_copy(
                src.at[pl.ds(q * QB, QB)], inbox.at[q], turn_recv.at[k, q]
            ).start()

    def turn_wait_recv(src, inbox, k, q):
        pltpu.make_async_copy(src.at[pl.ds(q * QB, QB)], inbox.at[q], turn_recv.at[k, q]).wait()

    def turn_wait_send(src, inbox, k):
        for q in range(NQ):

            @pl.when(jnp.logical_not(is_self(q)))
            def _():
                turn_copy(src, inbox, k, q).wait_send()

    def swap_matrices():
        n = PHASES * 8
        x, y = iota2((n, n), 0), iota2((n, n), 1)
        flipped = (x // PHASES) * PHASES + (x % STEP) * STEP + (x // STEP) % STEP
        phase = jnp.where(y == flipped, 1.0, 0.0).astype(BF16)
        m = 2 * L
        x, y = iota2((m, m), 0), iota2((m, m), 1)
        flipped = ((x // C) % 2) * L + (x // L) * C + x % C
        lanes = jnp.where(y == flipped, 1.0, 0.0).astype(BF16)
        return phase, lanes

    def turned(inbox, q, phase, lanes):
        got = inbox[q].reshape(nP, 2, nP, PHASES, L)
        pair = jnp.concatenate([got[:, 0], got[:, 1]], axis=-1).reshape(nP * nP * PHASES, 2 * L)
        swapped = dot(pair, lanes).astype(BF16)
        n = phase.shape[0]
        parts = [
            dot(phase, swapped[i * n : (i + 1) * n]).astype(BF16)
            for i in range(nP * nP * PHASES // n)
        ]
        return jnp.concatenate(parts, axis=0).reshape(nP, nP, PHASES, 2 * L)

    def halo_copy(img, k, n):
        dr, dc = DIRECTIONS[n]
        rows = {-1: (2, nI + 2, 2), 0: (2, 2, nI), 1: (nI, 0, 2)}[dr]
        cols = {-1: (1, nP + 1, 1), 0: (1, 1, nP), 1: (nP, 0, 1)}[dc]
        return pltpu.make_async_remote_copy(
            src_ref=img.at[pl.ds(rows[0], rows[2]), pl.ds(cols[0], cols[2])],
            dst_ref=img.at[pl.ds(rows[1], rows[2]), pl.ds(cols[1], cols[2])],
            send_sem=halo_send.at[k, n],
            recv_sem=halo_recv.at[k, n],
            device_id=(r + dr, c + dc),
            device_id_type=MESH,
        )

    def halo_start(img, k):
        for n in (2, 3, 4, 5, 6, 7, 0, 1):

            @pl.when(exists(DIRECTIONS[n]))
            def _():
                halo_copy(img, k, n).start()

    def halo_wait(img, k):
        for n, (dr, dc) in enumerate(DIRECTIONS):

            @pl.when(exists((-dr, -dc)))
            def _():
                halo_copy(img, k, n).wait_recv()

            @pl.when(exists((dr, dc)))
            def _():
                halo_copy(img, k, n).wait_send()

    def conv(src, k0, count, pairs, which):
        taps = []
        for dy in range(3):
            got = src[pl.ds(k0 + dy, count)]
            for side in range(2):
                taps.append(got[:, side : side + pairs].reshape(count * pairs * PHASES, L))
        return dot(jnp.concatenate(taps, axis=1), packed[which])

    def clear_outside(img):
        @pl.when(r == 0)
        def _():
            img[0] = jnp.zeros((nP + 1, PHASES, L), BF16)

        @pl.when(r == rows_axis - 1)
        def _():
            img[nI + 1] = jnp.zeros((nP + 1, PHASES, L), BF16)

        @pl.when(c == 0)
        def _():
            img[:, 0, :, 0:C] = jnp.zeros((nI + 2, PHASES, C), BF16)

        @pl.when(c == cols_axis - 1)
        def _():
            img[:, nP, :, C:L] = jnp.zeros((nI + 2, PHASES, C), BF16)

    enter(feature, own)
    pl.semaphore_wait(barrier, expected)
    for q in range(NQ):
        turn_start(own, inbox1, 0, q)

    enter(cotangent, cot)
    eye = jnp.where(iota2((C, C), 0) == iota2((C, C), 1), 1.0, 0.0).astype(BF16)
    nothing = jnp.zeros((C, C), BF16)
    for which, w, back in ((0, w_first, 0), (1, w_second, 0), (2, w_second, 1), (3, w_first, 1)):
        for dy in range(3):
            tap = [
                dot(eye, w[2 - dy, 2 - kx], NT).astype(BF16) if back else w[dy, kx]
                for kx in range(3)
            ]
            for a in range(4):
                left = tap[a] if a < 3 else nothing
                right = tap[a - 1] if a > 0 else nothing
                packed[which, pl.ds(dy * 4 * C + a * C, C)] = jnp.concatenate([left, right], axis=1)
    bias1 = jnp.concatenate([b_first[...], b_first[...]], axis=1)
    bias2 = jnp.concatenate([b_second[...], b_second[...]], axis=1)

    phase, lanes = swap_matrices()
    for q in range(NQ):
        turn_wait_recv(own, inbox1, 0, q)
        got = turned(inbox1, q, phase, lanes)
        for jp in range(nP):
            for b in range(2):
                i = q * QB + 2 * jp + b
                total = own[i].astype(F32) + got[:, jp, :, b * L : (b + 1) * L].astype(F32)
                sym[i + 2, 1 : nP + 1] = total.astype(BF16)

    halo_start(sym, 0)
    turn_wait_send(own, inbox1, 0)
    halo_wait(sym, 0)

    half = (nI + 2) // 2

    @pl.loop(0, 2)
    def _(t):
        k0 = t * half
        pre = conv(sym, k0, half, nP + 1, 0) + bias1
        value, rise = gelu_and_slope(pre)
        hid[pl.ds(k0, half)] = value.astype(BF16).reshape(half, nP + 1, PHASES, L)
        slope[pl.ds(k0, half)] = rise.reshape(half, nP + 1, PHASES, L)

    clear_outside(hid)

    @pl.loop(0, NQ)
    def _(t):
        k0 = t * QB
        pre = conv(hid, k0, QB, nP, 1) + bias2
        value, rise = gelu_and_slope(pre)
        size = (QB, nP, PHASES, L)
        base = sym[pl.ds(k0 + 2, QB)][:, 1 : nP + 1].astype(F32)
        fresh[pl.ds(k0, QB)] = (base + value.reshape(size)).astype(BF16)
        pull = cot[pl.ds(k0, QB)].astype(F32) * rise.reshape(size)
        g2[pl.ds(k0 + 2, QB), 1 : nP + 1] = pull.astype(BF16)

    halo_start(g2, 1)
    leave(fresh, out_ref)
    halo_wait(g2, 1)

    @pl.loop(0, 2)
    def _(t):
        k0 = t * half
        pulled = conv(g2, k0, half, nP + 1, 2).reshape(half, nP + 1, PHASES, L)
        g1[pl.ds(k0, half)] = (pulled * slope[pl.ds(k0, half)]).astype(BF16)

    clear_outside(g1)

    for q in range(NQ):
        k0 = q * QB
        total = conv(g1, k0, QB, nP, 3).reshape(QB, nP, PHASES, L)
        gsym[pl.ds(k0, QB)] = (cot[pl.ds(k0, QB)].astype(F32) + total).astype(BF16)
        turn_start(gsym, inbox2, 1, q)

    for q in range(NQ):
        turn_wait_recv(gsym, inbox2, 1, q)
        got = turned(inbox2, q, phase, lanes)
        for jp in range(nP):
            for b in range(2):
                i = q * QB + 2 * jp + b
                total = gsym[i].astype(F32) + got[:, jp, :, b * L : (b + 1) * L].astype(F32)
                fresh[i] = total.astype(BF16)
    turn_wait_send(gsym, inbox2, 1)
    leave(fresh, grad_ref)


def per_device(rows_axis, cols_axis, feature, w1, b1, w2, b2, cotangent):
    TR, TC, C = feature.shape
    nI, nP = TR // STEP, TC // (2 * STEP)
    QB, NQ, L = TC // STEP, TR // TC, 2 * C
    turned = lambda x: jnp.transpose(x, (1, 2, 0))
    image = lambda i, p: pltpu.VMEM((i, p, PHASES, L), BF16)
    vmem = pl.BlockSpec(memory_space=pltpu.VMEM)
    out = jax.ShapeDtypeStruct((TC, C, TR), BF16)
    res = pl.pallas_call(
        functools.partial(kernel, rows_axis, cols_axis),
        out_shape=(out, out),
        in_specs=[vmem] * 6,
        out_specs=(vmem, vmem),
        scratch_shapes=[
            pltpu.VMEM((nI * PHASES, STEP * TR), BF16),
            image(nI, nP),
            image(nI, nP),
            image(nI + 4, nP + 2),
            image(nI + 2, nP + 1),
            image(nI + 4, nP + 2),
            image(nI + 2, nP + 1),
            image(nI, nP),
            image(nI, nP),
            pltpu.VMEM((nI + 2, nP + 1, PHASES, L), F32),
            pltpu.VMEM((4, 12 * C, L), BF16),
            pltpu.VMEM((NQ, QB, nP, PHASES, L), BF16),
            pltpu.VMEM((NQ, QB, nP, PHASES, L), BF16),
            pltpu.SemaphoreType.DMA((2, 8)),
            pltpu.SemaphoreType.DMA((2, 8)),
            pltpu.SemaphoreType.DMA((2, NQ)),
            pltpu.SemaphoreType.DMA((2, NQ)),
        ],
        compiler_params=pltpu.CompilerParams(
            collective_id=0, has_side_effects=True, vmem_limit_bytes=60000000
        ),
    )(turned(feature), w1, b1.reshape(1, C), w2, b2.reshape(1, C), turned(cotangent))
    return tuple(jnp.transpose(x, (2, 0, 1)) for x in res)


def solution(mesh):
    specs = P("row", "col", None)
    return jax.shard_map(
        functools.partial(per_device, mesh.shape["row"], mesh.shape["col"]),
        mesh=mesh,
        in_specs=(specs, P(), P(), P(), P(), specs),
        out_specs=(specs, specs),
        check_vma=False,
    )
```

profile of v0, /device:TPU:77, one launch (start us, length us, event | category | flops | bytes accessed | tf_op | source)
XLA Modules:
  0.0 135.7 jit_solution(1147308119718175180)
XLA Ops:
  0.6 132.3 %shard_map.77 = (bf16[32,64,128]{2,1,0:T(8,128)(2,1)}, bf16[32,64,128]{2,1,0:T(8,128)(2,1)}) custom-call(bf16[32,64,128]{2,1,0:T(8,128)(2,1)} %bitcast.6, bf16[3,3,64,64]{3,2,1,0:T(8,128)(2,1)} %w_first.1, f32[1,64]{1,0:T(1,128)} %bitcast.10, bf16[3,3,64,64]{3,2,1,0:T(8,128)(2,1)} %w_second.1, f32[1,64]{1,0:T(1,128)} %bitcast.11, bf16[32,64,128]{2,1,0:T(8,128)(2,1)} %bitcast.7), custom_call_target="tpu_custom_call" | custom-call | tf_op jit(solution)/shard_map/pallas_call | solution.py:352
  132.9 0.0 copy-start
  132.9 1.9 %copy.10 = bf16[128,32,64]{0,2,1:T(8,128)(2,1)} copy(bf16[128,32,64]{0,2,1:T(8,128)(2,1)} %bitcast.9) | data formatting | bytes 1048576
  134.9 0.0 copy-done
  134.9 0.8 copy.11
Async XLA Ops:
  132.9 1.9 %copy-start = (bf16[32,64,128]{2,1,0:T(8,128)(2,1)S(1)}, bf16[32,64,128]{2,1,0:T(8,128)(2,1)}, u32[]{:S(2)}) copy-start(bf16[32,64,128]{2,1,0:T(8,128)(2,1)} %get-tuple-element.5) | copy-start | bytes 1572868
where the time goes:
time: 136 us
  Pallas kernels  132 us (97%)
  local copies, waits for them, and re-layouts  2.72 us (2%)
    pallas_call x1, Pallas kernels, per_device(): pl.pallas_call(functools.partial(kernel, rows_axis, cols_axis), out_shape...  132 us
    unnamed x4, local copies, waits for them, and re-layouts  2.72 us

commit v1 on v0

--- a/solution.py
+++ b/solution.py
@@ -14,6 +14,8 @@
 BF16 = jnp.bfloat16
 ROOT_HALF = 0.7071067811865476
 INV_ROOT_TAU = 0.3989422804014327
+RELAYED = 4
+SLOTS = 16
 DIRECTIONS = [(-1, 0), (1, 0), (0, -1), (0, 1), (-1, -1), (-1, 1), (1, -1), (1, 1)]
 NT = (((1,), (1,)), ((), ()))
 TN = (((0,), (0,)), ((), ()))
@@ -62,10 +64,14 @@
     packed,
     inbox1,
     inbox2,
+    relay1,
+    relay2,
     halo_send,
     halo_recv,
     turn_send,
     turn_recv,
+    relay_send,
+    relay_recv,
 ):
     C = w_first.shape[-1]
     TC, _, TR = feature.shape
@@ -80,6 +86,28 @@
 
     def is_self(q):
         return jnp.logical_and(c // NQ == r, r * NQ + q == c)
+
+    def same(a, b):
+        return jnp.logical_and(a[0] == b[0], a[1] == b[1])
+
+    me = (r, c)
+    relaying = jnp.logical_and(r // 4 == c // 16, (c % 8) // 4 == r % 2)
+
+    def relay_of(s, q):
+        return ((s[0] // 4) * 4 + (s[1] // 4) % 4, (s[0] // 2) * 8 + s[1] % 8)
+
+    def relay_slot(q):
+        return ((c // 16) * 2 + r % 2) * 4 + q
+
+    def slot_source(n):
+        x = 2 * (n // 8) + (r % 4) // 2
+        y = 2 * ((c // 8) % 2) + (n // 4) % 2
+        return ((r // 4) * 4 + y, x * 8 + c % 8), n % 4
+
+    relay_in = [((c // 16) * 4 + r % 4, (c // 8) * 8 + (r % 2) * 4 + k) for k in range(4)]
+    relay_out = [relay_of(me, 0)]
+    sources = [slot_source(n)[0] for n in range(0, SLOTS, 4)]
+    targets = 16
 
     def exists(d):
         dr, dc = d
@@ -110,6 +138,26 @@
         def _():
             pl.semaphore_signal(barrier, inc=1, device_id=partner(q), device_id_type=MESH)
 
+    def greet(other):
+        @pl.when(jnp.logical_not(same(other, me)))
+        def _():
+            pl.semaphore_signal(barrier, inc=1, device_id=other, device_id_type=MESH)
+
+    for other in relay_in:
+        greet(other)
+    for other in relay_out:
+        expected = expected + jnp.logical_not(same(other, me)).astype(jnp.int32)
+
+    @pl.when(relaying)
+    def _():
+        for other in sources:
+            greet(other)
+
+    greeted = jnp.int32(targets)
+    for other in relay_in:
+        greeted = greeted - same(other, me).astype(jnp.int32)
+    expected = expected + jnp.where(relaying, greeted, 0)
+
     for d in DIRECTIONS:
         here = exists(d)
         expected = expected + here.astype(jnp.int32)
@@ -142,38 +190,122 @@
                 for s in range(STEP):
                     dst[base + STEP * b + s] = res[b * C : (b + 1) * C, s * TR : (s + 1) * TR]
 
-    def turn_copy(src, inbox, k, q):
+    def by_relay(s, q):
+        w = relay_of(s, q)
+        t = (s[1] // NQ, s[0] * NQ + q)
+        return jnp.logical_not(jnp.logical_or(same(w, s), same(w, t)))
+
+    def part_rows(part):
+        return pl.ds(0, RELAYED) if part else pl.ds(RELAYED, QB - RELAYED)
+
+    def block(src, q, part):
+        start, size = (0, RELAYED) if part else (RELAYED, QB - RELAYED)
+        return src.at[pl.ds(q * QB + start, size)]
+
+    def direct_copy(src, inbox, k, q, part):
+        slot = lax.rem(c, NQ)
         return pltpu.make_async_remote_copy(
-            src_ref=src.at[pl.ds(q * QB, QB)],
-            dst_ref=inbox.at[lax.rem(c, NQ)],
-            send_sem=turn_send.at[k, q],
-            recv_sem=turn_recv.at[k, lax.rem(c, NQ)],
+            src_ref=block(src, q, part),
+            dst_ref=inbox.at[slot, part_rows(part)],
+            send_sem=turn_send.at[k, q, part],
+            recv_sem=turn_recv.at[k, slot, part],
             device_id=partner(q),
             device_id_type=MESH,
         )
 
-    def turn_start(src, inbox, k, q):
-        mine = is_self(q)
-
-        @pl.when(jnp.logical_not(mine))
-        def _():
-            turn_copy(src, inbox, k, q).start()
-
-        @pl.when(mine)
-        def _():
-            pltpu.make_async_copy(
-                src.at[pl.ds(q * QB, QB)], inbox.at[q], turn_recv.at[k, q]
-            ).start()
+    def first_copy(src, relay, k, q):
+        return pltpu.make_async_remote_copy(
+            src_ref=block(src, q, 1),
+            dst_ref=relay.at[relay_slot(q)],
+            send_sem=turn_send.at[k, q, 1],
+            recv_sem=relay_recv.at[k, relay_slot(q)],
+            device_id=relay_of(me, q),
+            device_id_type=MESH,
+        )
+
+    def onward_copy(inbox, relay, k, n):
+        s, q = slot_source(n)
+        slot = lax.rem(s[1], NQ)
+        return pltpu.make_async_remote_copy(
+            src_ref=relay.at[n],
+            dst_ref=inbox.at[slot, part_rows(1)],
+            send_sem=relay_send.at[k, n],
+            recv_sem=turn_recv.at[k, slot, 1],
+            device_id=(s[1] // NQ, s[0] * NQ + q),
+            device_id_type=MESH,
+        )
+
+    def local_copy(src, inbox, k, q, part):
+        return pltpu.make_async_copy(
+            block(src, q, part), inbox.at[q, part_rows(part)], turn_recv.at[k, q, part]
+        )
+
+    def own_relayed(q):
+        return jnp.logical_and(jnp.logical_not(is_self(q)), by_relay(me, q))
+
+    def own_direct(q):
+        return jnp.logical_and(jnp.logical_not(is_self(q)), jnp.logical_not(by_relay(me, q)))
+
+    def turn_start(src, inbox, relay, k, q):
+        @pl.when(own_relayed(q))
+        def _():
+            first_copy(src, relay, k, q).start()
+
+        @pl.when(own_direct(q))
+        def _():
+            direct_copy(src, inbox, k, q, 1).start()
+
+        @pl.when(jnp.logical_not(is_self(q)))
+        def _():
+            direct_copy(src, inbox, k, q, 0).start()
+
+        @pl.when(is_self(q))
+        def _():
+            for part in range(2):
+                local_copy(src, inbox, k, q, part).start()
+
+    def slot_used(n):
+        s, q = slot_source(n)
+        t = (s[1] // NQ, s[0] * NQ + q)
+        return jnp.logical_and(jnp.logical_not(same(s, t)), by_relay(s, q))
+
+    def turn_relay(inbox, relay, k):
+        @pl.when(relaying)
+        def _():
+            @pl.loop(0, SLOTS)
+            def _(n):
+                @pl.when(slot_used(n))
+                def _():
+                    copy = onward_copy(inbox, relay, k, n)
+                    pltpu.make_async_copy(relay.at[n], relay.at[n], relay_recv.at[k, n]).wait()
+                    copy.start()
 
     def turn_wait_recv(src, inbox, k, q):
-        pltpu.make_async_copy(src.at[pl.ds(q * QB, QB)], inbox.at[q], turn_recv.at[k, q]).wait()
-
-    def turn_wait_send(src, inbox, k):
+        for part in range(2):
+            local_copy(src, inbox, k, q, part).wait()
+
+    def turn_wait_send(src, inbox, relay, k):
         for q in range(NQ):
+
+            @pl.when(own_relayed(q))
+            def _():
+                first_copy(src, relay, k, q).wait_send()
+
+            @pl.when(own_direct(q))
+            def _():
+                direct_copy(src, inbox, k, q, 1).wait_send()
 
             @pl.when(jnp.logical_not(is_self(q)))
             def _():
-                turn_copy(src, inbox, k, q).wait_send()
+                direct_copy(src, inbox, k, q, 0).wait_send()
+
+        @pl.when(relaying)
+        def _():
+            @pl.loop(0, SLOTS)
+            def _(n):
+                @pl.when(slot_used(n))
+                def _():
+                    onward_copy(inbox, relay, k, n).wait_send()
 
     def swap_matrices():
         n = PHASES * 8
@@ -256,7 +388,8 @@
     enter(feature, own)
     pl.semaphore_wait(barrier, expected)
     for q in range(NQ):
-        turn_start(own, inbox1, 0, q)
+        turn_start(own, inbox1, relay1, 0, q)
+    turn_relay(inbox1, relay1, 0)
 
     enter(cotangent, cot)
     eye = jnp.where(iota2((C, C), 0) == iota2((C, C), 1), 1.0, 0.0).astype(BF16)
@@ -285,7 +418,7 @@
                 sym[i + 2, 1 : nP + 1] = total.astype(BF16)
 
     halo_start(sym, 0)
-    turn_wait_send(own, inbox1, 0)
+    turn_wait_send(own, inbox1, relay1, 0)
     halo_wait(sym, 0)
 
     half = (nI + 2) // 2
@@ -327,7 +460,8 @@
         k0 = q * QB
         total = conv(g1, k0, QB, nP, 3).reshape(QB, nP, PHASES, L)
         gsym[pl.ds(k0, QB)] = (cot[pl.ds(k0, QB)].astype(F32) + total).astype(BF16)
-        turn_start(gsym, inbox2, 1, q)
+        turn_start(gsym, inbox2, relay2, 1, q)
+    turn_relay(inbox2, relay2, 1)
 
     for q in range(NQ):
         turn_wait_recv(gsym, inbox2, 1, q)
@@ -337,7 +471,7 @@
                 i = q * QB + 2 * jp + b
                 total = gsym[i].astype(F32) + got[:, jp, :, b * L : (b + 1) * L].astype(F32)
                 fresh[i] = total.astype(BF16)
-    turn_wait_send(gsym, inbox2, 1)
+    turn_wait_send(gsym, inbox2, relay2, 1)
     leave(fresh, grad_ref)
 
 
@@ -368,10 +502,14 @@
             pltpu.VMEM((4, 12 * C, L), BF16),
             pltpu.VMEM((NQ, QB, nP, PHASES, L), BF16),
             pltpu.VMEM((NQ, QB, nP, PHASES, L), BF16),
+            pltpu.VMEM((SLOTS, RELAYED, nP, PHASES, L), BF16),
+            pltpu.VMEM((SLOTS, RELAYED, nP, PHASES, L), BF16),
             pltpu.SemaphoreType.DMA((2, 8)),
             pltpu.SemaphoreType.DMA((2, 8)),
-            pltpu.SemaphoreType.DMA((2, NQ)),
-            pltpu.SemaphoreType.DMA((2, NQ)),
+            pltpu.SemaphoreType.DMA((2, NQ, 2)),
+            pltpu.SemaphoreType.DMA((2, NQ, 2)),
+            pltpu.SemaphoreType.DMA((2, SLOTS)),
+            pltpu.SemaphoreType.DMA((2, SLOTS)),
         ],
         compiler_params=pltpu.CompilerParams(
             collective_id=0, has_side_effects=True, vmem_limit_bytes=60000000

time: 136 us -> 118 us (0.87)
  the two profiles are of different devices: /device:TPU:77 before, /device:TPU:61 now
where the time goes in v1:
time: 118 us
  Pallas kernels  115 us (97%)
  local copies, waits for them, and re-layouts  2.72 us (2%)
    pallas_call x1, Pallas kernels, per_device(): pl.pallas_call(functools.partial(kernel, rows_axis, cols_axis), out_shape...  115 us
    unnamed x4, local copies, waits for them, and re-layouts  2.72 us

profile of v1, /device:TPU:61, one launch (start us, length us, event | category | flops | bytes accessed | tf_op | source)
XLA Modules:
  0.0 118.1 jit_solution(4226634195470345212)
XLA Ops:
  0.6 114.8 %shard_map.77 = (bf16[32,64,128]{2,1,0:T(8,128)(2,1)}, bf16[32,64,128]{2,1,0:T(8,128)(2,1)}) custom-call(bf16[32,64,128]{2,1,0:T(8,128)(2,1)} %bitcast.6, bf16[3,3,64,64]{3,2,1,0:T(8,128)(2,1)} %w_first.1, f32[1,64]{1,0:T(1,128)} %bitcast.10, bf16[3,3,64,64]{3,2,1,0:T(8,128)(2,1)} %w_second.1, f32[1,64]{1,0:T(1,128)} %bitcast.11, bf16[32,64,128]{2,1,0:T(8,128)(2,1)} %bitcast.7), custom_call_target="tpu_custom_call" | custom-call | tf_op jit(solution)/shard_map/pallas_call | solution.py:486
  115.4 0.0 copy-start
  115.4 1.9 %copy.10 = bf16[128,32,64]{0,2,1:T(8,128)(2,1)} copy(bf16[128,32,64]{0,2,1:T(8,128)(2,1)} %bitcast.9) | data formatting | bytes 1048576
  117.3 0.0 copy-done
  117.3 0.8 copy.11
Async XLA Ops:
  115.4 1.9 %copy-start = (bf16[32,64,128]{2,1,0:T(8,128)(2,1)S(1)}, bf16[32,64,128]{2,1,0:T(8,128)(2,1)}, u32[]{:S(2)}) copy-start(bf16[32,64,128]{2,1,0:T(8,128)(2,1)} %get-tuple-element.5) | copy-start | bytes 1572868

commit v2 on v0

--- a/solution.py
+++ b/solution.py
@@ -14,6 +14,8 @@
 BF16 = jnp.bfloat16
 ROOT_HALF = 0.7071067811865476
 INV_ROOT_TAU = 0.3989422804014327
+SLOTS = 16
+ROUTES = ((1224305661, 568855674),)
 DIRECTIONS = [(-1, 0), (1, 0), (0, -1), (0, 1), (-1, -1), (-1, 1), (1, -1), (1, 1)]
 NT = (((1,), (1,)), ((), ()))
 TN = (((0,), (0,)), ((), ()))
@@ -62,10 +64,14 @@
     packed,
     inbox1,
     inbox2,
+    relay1,
+    relay2,
     halo_send,
     halo_recv,
     turn_send,
     turn_recv,
+    relay_send,
+    relay_recv,
 ):
     C = w_first.shape[-1]
     TC, _, TR = feature.shape
@@ -80,6 +86,48 @@
 
     def is_self(q):
         return jnp.logical_and(c // NQ == r, r * NQ + q == c)
+
+    def same(a, b):
+        return jnp.logical_and(a[0] == b[0], a[1] == b[1])
+
+    me = (r, c)
+
+    def via_xy(s, q):
+        return ((s[0] // 4) * 4 + (s[1] // 4) % 4, (s[0] // 2) * 8 + s[1] % 8)
+
+    def via_xy_slot(q):
+        return ((c // 16) * 2 + r % 2) * 4 + q
+
+    def via_xy_source(n):
+        x = 2 * (n // 8) + (r % 4) // 2
+        y = 2 * ((c // 8) % 2) + (n // 4) % 2
+        return ((r // 4) * 4 + y, x * 8 + c % 8), n % 4
+
+    kinds = [
+        (
+            via_xy,
+            via_xy_slot,
+            via_xy_source,
+            jnp.logical_and(r // 4 == c // 16, (c % 8) // 4 == r % 2),
+            [((c // 16) * 4 + r % 4, (c // 8) * 8 + (r % 2) * 4 + k) for k in range(4)],
+            [via_xy_source(n)[0] for n in range(0, SLOTS, 4)],
+            [via_xy(me, 0)],
+            16,
+            lambda m: ((m % 4) * 4 + m // 8, (m // 4) % 2),
+        ),
+    ]
+
+    def taken(kind, part, s, q):
+        x1, x0, y1, y0 = s[1] // 16, (s[1] // 8) % 2, (s[0] % 4) // 2, s[0] % 2
+        z2, z1, z0, q1 = (s[1] % 8) // 4, (s[1] // 2) % 2, s[0] // 4, q // 2
+        differ = lambda a, b: (a + b) % 2
+        at = y0 + 2 * z2 + 4 * differ(x1, z0) + 8 * differ(x0, y1) + 16 * differ(z1, q1)
+        words = [jnp.int32(word) for word in ROUTES[kind]]
+        word = words[part] if isinstance(part, int) else jnp.where(part == 0, *words)
+        w = kinds[kind][0](s, q)
+        target = (s[1] // NQ, s[0] * NQ + q)
+        aside = jnp.logical_not(jnp.logical_or(same(w, s), same(w, target)))
+        return jnp.logical_and(aside, lax.shift_right_logical(word, at) % 2 == 1)
 
     def exists(d):
         dr, dc = d
@@ -110,6 +158,25 @@
         def _():
             pl.semaphore_signal(barrier, inc=1, device_id=partner(q), device_id_type=MESH)
 
+    def greet(other):
+        @pl.when(jnp.logical_not(same(other, me)))
+        def _():
+            pl.semaphore_signal(barrier, inc=1, device_id=other, device_id_type=MESH)
+
+    for _, _, _, relaying, relays, sources, firsts, targets, _ in kinds:
+        greeted = jnp.int32(targets)
+        for other in relays:
+            greet(other)
+            greeted = greeted - same(other, me).astype(jnp.int32)
+        for other in firsts:
+            expected = expected + jnp.logical_not(same(other, me)).astype(jnp.int32)
+        expected = expected + jnp.where(relaying, greeted, 0)
+
+        @pl.when(relaying)
+        def _():
+            for other in sources:
+                greet(other)
+
     for d in DIRECTIONS:
         here = exists(d)
         expected = expected + here.astype(jnp.int32)
@@ -142,38 +209,121 @@
                 for s in range(STEP):
                     dst[base + STEP * b + s] = res[b * C : (b + 1) * C, s * TR : (s + 1) * TR]
 
-    def turn_copy(src, inbox, k, q):
+    half_rows = QB // 2
+
+    def part_rows(part):
+        return pl.ds(part * half_rows, half_rows)
+
+    def block(src, q, part):
+        return src.at[pl.ds(q * QB + part * half_rows, half_rows)]
+
+    def direct_copy(src, inbox, k, q, part):
+        slot = lax.rem(c, NQ)
         return pltpu.make_async_remote_copy(
-            src_ref=src.at[pl.ds(q * QB, QB)],
-            dst_ref=inbox.at[lax.rem(c, NQ)],
-            send_sem=turn_send.at[k, q],
-            recv_sem=turn_recv.at[k, lax.rem(c, NQ)],
+            src_ref=block(src, q, part),
+            dst_ref=inbox.at[slot, part_rows(part)],
+            send_sem=turn_send.at[k, q, part],
+            recv_sem=turn_recv.at[k, slot, part],
             device_id=partner(q),
             device_id_type=MESH,
         )
 
-    def turn_start(src, inbox, k, q):
-        mine = is_self(q)
-
-        @pl.when(jnp.logical_not(mine))
-        def _():
-            turn_copy(src, inbox, k, q).start()
-
-        @pl.when(mine)
-        def _():
-            pltpu.make_async_copy(
-                src.at[pl.ds(q * QB, QB)], inbox.at[q], turn_recv.at[k, q]
-            ).start()
+    def first_copy(src, relay, k, kind, q, part):
+        slot = kinds[kind][1](q)
+        return pltpu.make_async_remote_copy(
+            src_ref=block(src, q, part),
+            dst_ref=relay.at[kind, slot, part],
+            send_sem=turn_send.at[k, q, part],
+            recv_sem=relay_recv.at[k, kind, slot, part],
+            device_id=kinds[kind][0](me, q),
+            device_id_type=MESH,
+        )
+
+    def onward_copy(inbox, relay, k, kind, n, part):
+        s, q = kinds[kind][2](n)
+        slot = lax.rem(s[1], NQ)
+        return pltpu.make_async_remote_copy(
+            src_ref=relay.at[kind, n, part],
+            dst_ref=inbox.at[slot, part_rows(part)],
+            send_sem=relay_send.at[k, kind, n, part],
+            recv_sem=turn_recv.at[k, slot, part],
+            device_id=(s[1] // NQ, s[0] * NQ + q),
+            device_id_type=MESH,
+        )
+
+    def local_copy(src, inbox, k, q, part):
+        return pltpu.make_async_copy(
+            block(src, q, part), inbox.at[q, part_rows(part)], turn_recv.at[k, q, part]
+        )
+
+    def way(q, part):
+        by = [taken(kind, part, me, q) for kind in range(len(kinds))]
+        straight = jnp.logical_not(is_self(q))
+        for one in by:
+            straight = jnp.logical_and(straight, jnp.logical_not(one))
+        return by, straight
+
+    ways = {(q, part): way(q, part) for q in range(NQ) for part in range(2)}
+
+    def turn_start(src, inbox, relay, k, qs):
+        for q in qs:
+            for part in range(2):
+                for kind, one in enumerate(ways[q, part][0]):
+
+                    @pl.when(one)
+                    def _():
+                        first_copy(src, relay, k, kind, q, part).start()
+
+        for q in qs:
+            for part in range(2):
+
+                @pl.when(ways[q, part][1])
+                def _():
+                    direct_copy(src, inbox, k, q, part).start()
+
+            @pl.when(is_self(q))
+            def _():
+                for part in range(2):
+                    local_copy(src, inbox, k, q, part).start()
+
+    def slots_do(act):
+        for kind, entry_of in enumerate(kinds):
+
+            @pl.when(entry_of[3])
+            def _():
+                @pl.loop(0, 2 * SLOTS)
+                def _(m):
+                    n, part = entry_of[-1](m)
+                    s, q = entry_of[2](n)
+
+                    @pl.when(taken(kind, part, s, q))
+                    def _():
+                        act(kind, n, part)
+
+    def turn_relay(inbox, relay, k):
+        def act(kind, n, part):
+            at = relay.at[kind, n, part]
+            pltpu.make_async_copy(at, at, relay_recv.at[k, kind, n, part]).wait()
+            onward_copy(inbox, relay, k, kind, n, part).start()
+
+        slots_do(act)
 
     def turn_wait_recv(src, inbox, k, q):
-        pltpu.make_async_copy(src.at[pl.ds(q * QB, QB)], inbox.at[q], turn_recv.at[k, q]).wait()
-
-    def turn_wait_send(src, inbox, k):
+        for part in range(2):
+            local_copy(src, inbox, k, q, part).wait()
+
+    def turn_wait_send(src, inbox, relay, k):
         for q in range(NQ):
-
-            @pl.when(jnp.logical_not(is_self(q)))
-            def _():
-                turn_copy(src, inbox, k, q).wait_send()
+            for part in range(2):
+
+                @pl.when(jnp.logical_not(is_self(q)))
+                def _():
+                    direct_copy(src, inbox, k, q, part).wait_send()
+
+        def act(kind, n, part):
+            onward_copy(inbox, relay, k, kind, n, part).wait_send()
+
+        slots_do(act)
 
     def swap_matrices():
         n = PHASES * 8
@@ -255,8 +405,8 @@
 
     enter(feature, own)
     pl.semaphore_wait(barrier, expected)
-    for q in range(NQ):
-        turn_start(own, inbox1, 0, q)
+    turn_start(own, inbox1, relay1, 0, range(NQ))
+    turn_relay(inbox1, relay1, 0)
 
     enter(cotangent, cot)
     eye = jnp.where(iota2((C, C), 0) == iota2((C, C), 1), 1.0, 0.0).astype(BF16)
@@ -285,7 +435,7 @@
                 sym[i + 2, 1 : nP + 1] = total.astype(BF16)
 
     halo_start(sym, 0)
-    turn_wait_send(own, inbox1, 0)
+    turn_wait_send(own, inbox1, relay1, 0)
     halo_wait(sym, 0)
 
     half = (nI + 2) // 2
@@ -327,7 +477,8 @@
         k0 = q * QB
         total = conv(g1, k0, QB, nP, 3).reshape(QB, nP, PHASES, L)
         gsym[pl.ds(k0, QB)] = (cot[pl.ds(k0, QB)].astype(F32) + total).astype(BF16)
-        turn_start(gsym, inbox2, 1, q)
+        turn_start(gsym, inbox2, relay2, 1, [q])
+    turn_relay(inbox2, relay2, 1)
 
     for q in range(NQ):
         turn_wait_recv(gsym, inbox2, 1, q)
@@ -337,7 +488,7 @@
                 i = q * QB + 2 * jp + b
                 total = gsym[i].astype(F32) + got[:, jp, :, b * L : (b + 1) * L].astype(F32)
                 fresh[i] = total.astype(BF16)
-    turn_wait_send(gsym, inbox2, 1)
+    turn_wait_send(gsym, inbox2, relay2, 1)
     leave(fresh, grad_ref)
 
 
@@ -368,10 +519,14 @@
             pltpu.VMEM((4, 12 * C, L), BF16),
             pltpu.VMEM((NQ, QB, nP, PHASES, L), BF16),
             pltpu.VMEM((NQ, QB, nP, PHASES, L), BF16),
+            pltpu.VMEM((len(ROUTES), SLOTS, 2, QB // 2, nP, PHASES, L), BF16),
+            pltpu.VMEM((len(ROUTES), SLOTS, 2, QB // 2, nP, PHASES, L), BF16),
             pltpu.SemaphoreType.DMA((2, 8)),
             pltpu.SemaphoreType.DMA((2, 8)),
-            pltpu.SemaphoreType.DMA((2, NQ)),
-            pltpu.SemaphoreType.DMA((2, NQ)),
+            pltpu.SemaphoreType.DMA((2, NQ, 2)),
+            pltpu.SemaphoreType.DMA((2, NQ, 2)),
+            pltpu.SemaphoreType.DMA((2, len(ROUTES), SLOTS, 2)),
+            pltpu.SemaphoreType.DMA((2, len(ROUTES), SLOTS, 2)),
         ],
         compiler_params=pltpu.CompilerParams(
             collective_id=0, has_side_effects=True, vmem_limit_bytes=60000000

time: 136 us -> 95.2 us (0.70)
  the two profiles are of different devices: /device:TPU:77 before, /device:TPU:117 now
where the time goes in v2:
time: 95.2 us; the launch traced here: 95.1 us
  Pallas kernels  91.7 us (96%)
  local copies, waits for them, and re-layouts  2.72 us (3%)
    pallas_call x1, Pallas kernels, per_device(): pl.pallas_call(functools.partial(kernel, rows_axis, cols_axis), out_shape...  91.7 us
    unnamed x4, local copies, waits for them, and re-layouts  2.72 us

profile of v2, /device:TPU:117, one launch (start us, length us, event | category | flops | bytes accessed | tf_op | source)
XLA Modules:
  0.0 95.1 jit_solution(1643513840143710858)
XLA Ops:
  0.6 91.7 %shard_map.77 = (bf16[32,64,128]{2,1,0:T(8,128)(2,1)}, bf16[32,64,128]{2,1,0:T(8,128)(2,1)}) custom-call(bf16[32,64,128]{2,1,0:T(8,128)(2,1)} %bitcast.6, bf16[3,3,64,64]{3,2,1,0:T(8,128)(2,1)} %w_first.1, f32[1,64]{1,0:T(1,128)} %bitcast.10, bf16[3,3,64,64]{3,2,1,0:T(8,128)(2,1)} %w_second.1, f32[1,64]{1,0:T(1,128)} %bitcast.11, bf16[32,64,128]{2,1,0:T(8,128)(2,1)} %bitcast.7), custom_call_target="tpu_custom_call" | custom-call | tf_op jit(solution)/shard_map/pallas_call | solution.py:503
  92.4 0.0 copy-start
  92.4 1.9 %copy.10 = bf16[128,32,64]{0,2,1:T(8,128)(2,1)} copy(bf16[128,32,64]{0,2,1:T(8,128)(2,1)} %bitcast.9) | data formatting | bytes 1048576
  94.3 0.0 copy-done
  94.3 0.8 copy.11
Async XLA Ops:
  92.4 1.9 %copy-start = (bf16[32,64,128]{2,1,0:T(8,128)(2,1)S(1)}, bf16[32,64,128]{2,1,0:T(8,128)(2,1)}, u32[]{:S(2)}) copy-start(bf16[32,64,128]{2,1,0:T(8,128)(2,1)} %get-tuple-element.5) | copy-start | bytes 1572868

commit v3 on v2

--- a/solution.py
+++ b/solution.py
@@ -15,6 +15,7 @@
 ROOT_HALF = 0.7071067811865476
 INV_ROOT_TAU = 0.3989422804014327
 SLOTS = 16
+PARTS = 1
 ROUTES = ((1224305661, 568855674),)
 DIRECTIONS = [(-1, 0), (1, 0), (0, -1), (0, 1), (-1, -1), (-1, 1), (1, -1), (1, 1)]
 NT = (((1,), (1,)), ((), ()))
@@ -43,14 +44,21 @@
 def kernel(
     rows_axis,
     cols_axis,
+    feature_hbm,
+    w_first_hbm,
+    b_first_hbm,
+    w_second_hbm,
+    b_second_hbm,
+    cotangent_hbm,
+    out_ref,
+    grad_ref,
     feature,
     w_first,
     b_first,
     w_second,
     b_second,
     cotangent,
-    out_ref,
-    grad_ref,
+    load_sem,
     entry,
     own,
     cot,
@@ -113,7 +121,7 @@
             [via_xy_source(n)[0] for n in range(0, SLOTS, 4)],
             [via_xy(me, 0)],
             16,
-            lambda m: ((m % 4) * 4 + m // 8, (m // 4) % 2),
+            lambda m: ((m % 4) * 4 + m // (4 * PARTS), (m // 4) % PARTS),
         ),
     ]
 
@@ -123,7 +131,7 @@
         differ = lambda a, b: (a + b) % 2
         at = y0 + 2 * z2 + 4 * differ(x1, z0) + 8 * differ(x0, y1) + 16 * differ(z1, q1)
         words = [jnp.int32(word) for word in ROUTES[kind]]
-        word = words[part] if isinstance(part, int) else jnp.where(part == 0, *words)
+        word = words[q % 2] if isinstance(q, int) else jnp.where(q % 2 == 0, *words)
         w = kinds[kind][0](s, q)
         target = (s[1] // NQ, s[0] * NQ + q)
         aside = jnp.logical_not(jnp.logical_or(same(w, s), same(w, target)))
@@ -142,6 +150,22 @@
             ok = cond if ok is None else jnp.logical_and(ok, cond)
         return ok
 
+    loads = [
+        pltpu.make_async_copy(a, b, load_sem.at[i])
+        for i, (a, b) in enumerate(
+            (
+                (feature_hbm, feature),
+                (cotangent_hbm, cotangent),
+                (w_first_hbm, w_first),
+                (w_second_hbm, w_second),
+                (b_first_hbm, b_first),
+                (b_second_hbm, b_second),
+            )
+        )
+    ]
+    for load in loads:
+        load.start()
+
     for img in (sym, g2):
         img[0:2] = jnp.zeros((2, nP + 2, PHASES, L), BF16)
         img[nI + 2 : nI + 4] = jnp.zeros((2, nP + 2, PHASES, L), BF16)
@@ -209,7 +233,7 @@
                 for s in range(STEP):
                     dst[base + STEP * b + s] = res[b * C : (b + 1) * C, s * TR : (s + 1) * TR]
 
-    half_rows = QB // 2
+    half_rows = QB // PARTS
 
     def part_rows(part):
         return pl.ds(part * half_rows, half_rows)
@@ -263,11 +287,11 @@
             straight = jnp.logical_and(straight, jnp.logical_not(one))
         return by, straight
 
-    ways = {(q, part): way(q, part) for q in range(NQ) for part in range(2)}
+    ways = {(q, part): way(q, part) for q in range(NQ) for part in range(PARTS)}
 
     def turn_start(src, inbox, relay, k, qs):
         for q in qs:
-            for part in range(2):
+            for part in range(PARTS):
                 for kind, one in enumerate(ways[q, part][0]):
 
                     @pl.when(one)
@@ -275,7 +299,7 @@
                         first_copy(src, relay, k, kind, q, part).start()
 
         for q in qs:
-            for part in range(2):
+            for part in range(PARTS):
 
                 @pl.when(ways[q, part][1])
                 def _():
@@ -283,22 +307,19 @@
 
             @pl.when(is_self(q))
             def _():
-                for part in range(2):
+                for part in range(PARTS):
                     local_copy(src, inbox, k, q, part).start()
 
     def slots_do(act):
-        for kind, entry_of in enumerate(kinds):
-
-            @pl.when(entry_of[3])
-            def _():
-                @pl.loop(0, 2 * SLOTS)
-                def _(m):
-                    n, part = entry_of[-1](m)
-                    s, q = entry_of[2](n)
-
-                    @pl.when(taken(kind, part, s, q))
-                    def _():
-                        act(kind, n, part)
+        @pl.loop(0, PARTS * SLOTS)
+        def _(m):
+            for kind, entry_of in enumerate(kinds):
+                n, part = entry_of[-1](m)
+                s, q = entry_of[2](n)
+
+                @pl.when(jnp.logical_and(entry_of[3], taken(kind, part, s, q)))
+                def _():
+                    act(kind, n, part)
 
     def turn_relay(inbox, relay, k):
         def act(kind, n, part):
@@ -309,12 +330,12 @@
         slots_do(act)
 
     def turn_wait_recv(src, inbox, k, q):
-        for part in range(2):
+        for part in range(PARTS):
             local_copy(src, inbox, k, q, part).wait()
 
     def turn_wait_send(src, inbox, relay, k):
         for q in range(NQ):
-            for part in range(2):
+            for part in range(PARTS):
 
                 @pl.when(jnp.logical_not(is_self(q)))
                 def _():
@@ -347,9 +368,13 @@
         ]
         return jnp.concatenate(parts, axis=0).reshape(nP, nP, PHASES, 2 * L)
 
+    pieces = [(-1, 0, 0), (-1, -1, 0), (-1, 1, 0), (1, 0, 0), (1, -1, 0), (1, 1, 0)]
+    pieces += [(0, dc, part) for part in range(2) for dc in (-1, 1)]
+
     def halo_copy(img, k, n):
-        dr, dc = DIRECTIONS[n]
-        rows = {-1: (2, nI + 2, 2), 0: (2, 2, nI), 1: (nI, 0, 2)}[dr]
+        dr, dc, part = pieces[n]
+        half = nI // 2
+        rows = {-1: (2, nI + 2, 2), 0: (2 + part * half,) * 2 + (half,), 1: (nI, 0, 2)}[dr]
         cols = {-1: (1, nP + 1, 1), 0: (1, 1, nP), 1: (nP, 0, 1)}[dc]
         return pltpu.make_async_remote_copy(
             src_ref=img.at[pl.ds(rows[0], rows[2]), pl.ds(cols[0], cols[2])],
@@ -360,15 +385,16 @@
             device_id_type=MESH,
         )
 
-    def halo_start(img, k):
-        for n in (2, 3, 4, 5, 6, 7, 0, 1):
-
-            @pl.when(exists(DIRECTIONS[n]))
+    def halo_start(img, k, q):
+        last = {0: (0, 1, 2), NQ // 2 - 1: (6, 7), NQ - 1: (8, 9, 3, 4, 5)}
+        for n in last.get(q, ()):
+
+            @pl.when(exists(pieces[n][:2]))
             def _():
                 halo_copy(img, k, n).start()
 
     def halo_wait(img, k):
-        for n, (dr, dc) in enumerate(DIRECTIONS):
+        for n, (dr, dc, _) in enumerate(pieces):
 
             @pl.when(exists((-dr, -dc)))
             def _():
@@ -378,14 +404,17 @@
             def _():
                 halo_copy(img, k, n).wait_send()
 
-    def conv(src, k0, count, pairs, which):
+    def conv(src, k0, count, p0, pairs, which):
         taps = []
         for dy in range(3):
-            got = src[pl.ds(k0 + dy, count)]
+            got = src[pl.ds(k0 + dy, count), p0 : p0 + pairs + 1]
             for side in range(2):
                 taps.append(got[:, side : side + pairs].reshape(count * pairs * PHASES, L))
         return dot(jnp.concatenate(taps, axis=1), packed[which])
 
+    inside = [(2 + t * (nI - 2) // 2, (nI - 2) // 2, 1, nP - 1) for t in range(2)]
+    around = [(0, 2, 0, nP + 1), (nI, 2, 0, nP + 1), (2, nI - 2, 0, 1), (2, nI - 2, nP, 1)]
+
     def clear_outside(img):
         @pl.when(r == 0)
         def _():
@@ -403,11 +432,14 @@
         def _():
             img[:, nP, :, C:L] = jnp.zeros((nI + 2, PHASES, C), BF16)
 
+    loads[0].wait()
     enter(feature, own)
     pl.semaphore_wait(barrier, expected)
     turn_start(own, inbox1, relay1, 0, range(NQ))
     turn_relay(inbox1, relay1, 0)
 
+    for load in loads[1:]:
+        load.wait()
     enter(cotangent, cot)
     eye = jnp.where(iota2((C, C), 0) == iota2((C, C), 1), 1.0, 0.0).astype(BF16)
     nothing = jnp.zeros((C, C), BF16)
@@ -433,49 +465,52 @@
                 i = q * QB + 2 * jp + b
                 total = own[i].astype(F32) + got[:, jp, :, b * L : (b + 1) * L].astype(F32)
                 sym[i + 2, 1 : nP + 1] = total.astype(BF16)
-
-    halo_start(sym, 0)
+        halo_start(sym, 0, q)
+
+    def first_layer(k0, count, p0, pairs):
+        pre = conv(sym, k0, count, p0, pairs, 0) + bias1
+        value, rise = gelu_and_slope(pre)
+        size = (count, pairs, PHASES, L)
+        hid[pl.ds(k0, count), p0 : p0 + pairs] = value.astype(BF16).reshape(size)
+        slope[pl.ds(k0, count), p0 : p0 + pairs] = rise.reshape(size)
+
+    for box in inside:
+        first_layer(*box)
     turn_wait_send(own, inbox1, relay1, 0)
     halo_wait(sym, 0)
-
-    half = (nI + 2) // 2
-
-    @pl.loop(0, 2)
-    def _(t):
-        k0 = t * half
-        pre = conv(sym, k0, half, nP + 1, 0) + bias1
-        value, rise = gelu_and_slope(pre)
-        hid[pl.ds(k0, half)] = value.astype(BF16).reshape(half, nP + 1, PHASES, L)
-        slope[pl.ds(k0, half)] = rise.reshape(half, nP + 1, PHASES, L)
-
+    for box in around:
+        first_layer(*box)
     clear_outside(hid)
 
-    @pl.loop(0, NQ)
-    def _(t):
-        k0 = t * QB
-        pre = conv(hid, k0, QB, nP, 1) + bias2
+    for q in range(NQ):
+        k0 = q * QB
+        pre = conv(hid, k0, QB, 0, nP, 1) + bias2
         value, rise = gelu_and_slope(pre)
         size = (QB, nP, PHASES, L)
-        base = sym[pl.ds(k0 + 2, QB)][:, 1 : nP + 1].astype(F32)
+        base = sym[pl.ds(k0 + 2, QB), 1 : nP + 1].astype(F32)
         fresh[pl.ds(k0, QB)] = (base + value.reshape(size)).astype(BF16)
         pull = cot[pl.ds(k0, QB)].astype(F32) * rise.reshape(size)
         g2[pl.ds(k0 + 2, QB), 1 : nP + 1] = pull.astype(BF16)
-
-    halo_start(g2, 1)
+        halo_start(g2, 1, q)
+
+    def first_pull(k0, count, p0, pairs):
+        size = (count, pairs, PHASES, L)
+        pulled = conv(g2, k0, count, p0, pairs, 2).reshape(size)
+        rise = slope[pl.ds(k0, count), p0 : p0 + pairs]
+        g1[pl.ds(k0, count), p0 : p0 + pairs] = (pulled * rise).astype(BF16)
+
+    for box in inside:
+        first_pull(*box)
     leave(fresh, out_ref)
     halo_wait(g2, 1)
-
-    @pl.loop(0, 2)
-    def _(t):
-        k0 = t * half
-        pulled = conv(g2, k0, half, nP + 1, 2).reshape(half, nP + 1, PHASES, L)
-        g1[pl.ds(k0, half)] = (pulled * slope[pl.ds(k0, half)]).astype(BF16)
+    for box in around:
+        first_pull(*box)
 
     clear_outside(g1)
 
     for q in range(NQ):
         k0 = q * QB
-        total = conv(g1, k0, QB, nP, 3).reshape(QB, nP, PHASES, L)
+        total = conv(g1, k0, QB, 0, nP, 3).reshape(QB, nP, PHASES, L)
         gsym[pl.ds(k0, QB)] = (cot[pl.ds(k0, QB)].astype(F32) + total).astype(BF16)
         turn_start(gsym, inbox2, relay2, 1, [q])
     turn_relay(inbox2, relay2, 1)
@@ -503,9 +538,16 @@
     res = pl.pallas_call(
         functools.partial(kernel, rows_axis, cols_axis),
         out_shape=(out, out),
-        in_specs=[vmem] * 6,
+        in_specs=[pl.BlockSpec(memory_space=pltpu.HBM)] * 6,
         out_specs=(vmem, vmem),
         scratch_shapes=[
+            pltpu.VMEM((TC, C, TR), BF16),
+            pltpu.VMEM(w1.shape, BF16),
+            pltpu.VMEM((1, C), F32),
+            pltpu.VMEM(w2.shape, BF16),
+            pltpu.VMEM((1, C), F32),
+            pltpu.VMEM((TC, C, TR), BF16),
+            pltpu.SemaphoreType.DMA((6,)),
             pltpu.VMEM((nI * PHASES, STEP * TR), BF16),
             image(nI, nP),
             image(nI, nP),
@@ -519,14 +561,14 @@
             pltpu.VMEM((4, 12 * C, L), BF16),
             pltpu.VMEM((NQ, QB, nP, PHASES, L), BF16),
             pltpu.VMEM((NQ, QB, nP, PHASES, L), BF16),
-            pltpu.VMEM((len(ROUTES), SLOTS, 2, QB // 2, nP, PHASES, L), BF16),
-            pltpu.VMEM((len(ROUTES), SLOTS, 2, QB // 2, nP, PHASES, L), BF16),
-            pltpu.SemaphoreType.DMA((2, 8)),
-            pltpu.SemaphoreType.DMA((2, 8)),
-            pltpu.SemaphoreType.DMA((2, NQ, 2)),
-            pltpu.SemaphoreType.DMA((2, NQ, 2)),
-            pltpu.SemaphoreType.DMA((2, len(ROUTES), SLOTS, 2)),
-            pltpu.SemaphoreType.DMA((2, len(ROUTES), SLOTS, 2)),
+            pltpu.VMEM((len(ROUTES), SLOTS, PARTS, QB // PARTS, nP, PHASES, L), BF16),
+            pltpu.VMEM((len(ROUTES), SLOTS, PARTS, QB // PARTS, nP, PHASES, L), BF16),
+            pltpu.SemaphoreType.DMA((2, 10)),
+            pltpu.SemaphoreType.DMA((2, 10)),
+            pltpu.SemaphoreType.DMA((2, NQ, PARTS)),
+            pltpu.SemaphoreType.DMA((2, NQ, PARTS)),
+            pltpu.SemaphoreType.DMA((2, len(ROUTES), SLOTS, PARTS)),
+            pltpu.SemaphoreType.DMA((2, len(ROUTES), SLOTS, PARTS)),
         ],
         compiler_params=pltpu.CompilerParams(
             collective_id=0, has_side_effects=True, vmem_limit_bytes=60000000

time: 95.2 us -> 91.9 us (0.965)
  the two profiles are of different devices: /device:TPU:117 before, /device:TPU:106 now
where the time goes in v3:
time: 91.9 us; the launch traced here: 91.8 us
  Pallas kernels  88.4 us (96%)
  local copies, waits for them, and re-layouts  2.72 us (3%)
    pallas_call x1, Pallas kernels, per_device(): pl.pallas_call(functools.partial(kernel, rows_axis, cols_axis), out_shape...  88.4 us
    unnamed x4, local copies, waits for them, and re-layouts  2.72 us

profile of v3, /device:TPU:106, one launch (start us, length us, event | category | flops | bytes accessed | tf_op | source)
XLA Modules:
  0.0 91.8 jit_solution(5171876981501002781)
XLA Ops:
  0.6 88.4 %shard_map.77 = (bf16[32,64,128]{2,1,0:T(8,128)(2,1)}, bf16[32,64,128]{2,1,0:T(8,128)(2,1)}) custom-call(bf16[32,64,128]{2,1,0:T(8,128)(2,1)} %bitcast.6, bf16[3,3,64,64]{3,2,1,0:T(8,128)(2,1)} %w_first_hbm.1, f32[1,64]{1,0:T(1,128)} %bitcast.10, bf16[3,3,64,64]{3,2,1,0:T(8,128)(2,1)} %w_second_hbm.1, f32[1,64]{1,0:T(1,128)} %bitcast.11, ...), custom_call_target="tpu_custom_call" | custom-call | tf_op jit(solution)/shard_map/pallas_call | solution.py:538
  89.0 0.0 copy-start
  89.0 1.9 %copy.10 = bf16[128,32,64]{0,2,1:T(8,128)(2,1)} copy(bf16[128,32,64]{0,2,1:T(8,128)(2,1)} %bitcast.9) | data formatting | bytes 1048576
  91.0 0.0 copy-done
  91.0 0.8 copy.11
Async XLA Ops:
  89.0 1.9 %copy-start = (bf16[32,64,128]{2,1,0:T(8,128)(2,1)S(1)}, bf16[32,64,128]{2,1,0:T(8,128)(2,1)}, u32[]{:S(2)}) copy-start(bf16[32,64,128]{2,1,0:T(8,128)(2,1)} %get-tuple-element.5) | copy-start | bytes 1572868

commit v4 on v3

--- a/solution.py
+++ b/solution.py
@@ -16,7 +16,7 @@
 INV_ROOT_TAU = 0.3989422804014327
 SLOTS = 16
 PARTS = 1
-ROUTES = ((1224305661, 568855674),)
+ROUTES = ((-638580491, 548734887),)
 DIRECTIONS = [(-1, 0), (1, 0), (0, -1), (0, 1), (-1, -1), (-1, 1), (1, -1), (1, 1)]
 NT = (((1,), (1,)), ((), ()))
 TN = (((0,), (0,)), ((), ()))
@@ -129,7 +129,7 @@
         x1, x0, y1, y0 = s[1] // 16, (s[1] // 8) % 2, (s[0] % 4) // 2, s[0] % 2
         z2, z1, z0, q1 = (s[1] % 8) // 4, (s[1] // 2) % 2, s[0] // 4, q // 2
         differ = lambda a, b: (a + b) % 2
-        at = y0 + 2 * z2 + 4 * differ(x1, z0) + 8 * differ(x0, y1) + 16 * differ(z1, q1)
+        at = z1 + 2 * q1 + 4 * differ(x1, z0) + 8 * differ(x0, y1) + 16 * differ(y0, z2)
         words = [jnp.int32(word) for word in ROUTES[kind]]
         word = words[q % 2] if isinstance(q, int) else jnp.where(q % 2 == 0, *words)
         w = kinds[kind][0](s, q)

time: 91.9 us -> 87.6 us (0.953)
  the two profiles are of different devices: /device:TPU:106 before, /device:TPU:117 now
where the time goes in v4:
time: 87.6 us; the launch traced here: 86.4 us
  Pallas kernels  83 us (95%)
  local copies, waits for them, and re-layouts  2.72 us (3%)
    pallas_call x1, Pallas kernels, per_device(): pl.pallas_call(functools.partial(kernel, rows_axis, cols_axis), out_shape...  83 us
    unnamed x4, local copies, waits for them, and re-layouts  2.72 us

profile of v4, /device:TPU:117, one launch (start us, length us, event | category | flops | bytes accessed | tf_op | source)
XLA Modules:
  0.0 86.4 jit_solution(3176609836532363192)
XLA Ops:
  0.6 83.0 %shard_map.77 = (bf16[32,64,128]{2,1,0:T(8,128)(2,1)}, bf16[32,64,128]{2,1,0:T(8,128)(2,1)}) custom-call(bf16[32,64,128]{2,1,0:T(8,128)(2,1)} %bitcast.6, bf16[3,3,64,64]{3,2,1,0:T(8,128)(2,1)} %w_first_hbm.1, f32[1,64]{1,0:T(1,128)} %bitcast.10, bf16[3,3,64,64]{3,2,1,0:T(8,128)(2,1)} %w_second_hbm.1, f32[1,64]{1,0:T(1,128)} %bitcast.11, ...), custom_call_target="tpu_custom_call" | custom-call | tf_op jit(solution)/shard_map/pallas_call | solution.py:538
  83.6 0.0 copy-start
  83.6 1.9 %copy.10 = bf16[128,32,64]{0,2,1:T(8,128)(2,1)} copy(bf16[128,32,64]{0,2,1:T(8,128)(2,1)} %bitcast.9) | data formatting | bytes 1048576
  85.6 0.0 copy-done
  85.6 0.8 copy.11
Async XLA Ops:
  83.6 1.9 %copy-start = (bf16[32,64,128]{2,1,0:T(8,128)(2,1)S(1)}, bf16[32,64,128]{2,1,0:T(8,128)(2,1)}, u32[]{:S(2)}) copy-start(bf16[32,64,128]{2,1,0:T(8,128)(2,1)} %get-tuple-element.5) | copy-start | bytes 1572868

commit v5 on v4

--- a/solution.py
+++ b/solution.py
@@ -571,9 +571,21 @@
             pltpu.SemaphoreType.DMA((2, len(ROUTES), SLOTS, PARTS)),
         ],
         compiler_params=pltpu.CompilerParams(
-            collective_id=0, has_side_effects=True, vmem_limit_bytes=60000000
+            collective_id=0, has_side_effects=True, vmem_limit_bytes=30000000
         ),
-    )(turned(feature), w1, b1.reshape(1, C), w2, b2.reshape(1, C), turned(cotangent))
+    )(
+        *(
+            pltpu.with_memory_space_constraint(x, pltpu.HBM)
+            for x in (
+                turned(feature),
+                w1,
+                b1.reshape(1, C),
+                w2,
+                b2.reshape(1, C),
+                turned(cotangent),
+            )
+        )
+    )
     return tuple(jnp.transpose(x, (2, 0, 1)) for x in res)
 
 

time: 87.6 us -> 85.6 us (0.977)
  local copies, waits for them, and re-layouts: 2.72 us -> 1.59 us
    unnamed x4 -> x2, local copies, waits for them, and re-layouts: 2.72 us -> 1.59 us
where the time goes in v5:
time: 85.6 us; the launch traced here: 84.4 us
  Pallas kernels  82.2 us (96%)
  local copies, waits for them, and re-layouts  1.59 us (2%)
    pallas_call x1, Pallas kernels, per_device(): pl.pallas_call(functools.partial(kernel, rows_axis, cols_axis), out_shape...  82.2 us

profile of v5, /device:TPU:117, one launch (start us, length us, event | category | flops | bytes accessed | tf_op | source)
XLA Modules:
  0.0 84.4 jit_solution(816473259348102843)
XLA Ops:
  0.6 82.2 %shard_map.77 = (bf16[32,64,128]{2,1,0:T(8,128)(2,1)S(1)}, bf16[32,64,128]{2,1,0:T(8,128)(2,1)S(1)}) custom-call(bf16[32,64,128]{2,1,0:T(8,128)(2,1)} %bitcast.8, bf16[3,3,64,64]{3,2,1,0:T(8,128)(2,1)} %w_first_hbm.1, f32[1,64]{1,0:T(1,128)} %bitcast.10, bf16[3,3,64,64]{3,2,1,0:T(8,128)(2,1)} %w_second_hbm.1, f32[1,64]{1,0:T(1,128)} %bitcast.11, ...), custom_call_target="tpu_custom_call" | custom-call | tf_op jit(solution)/shard_map/pallas_call | solution.py:538
  82.8 0.8 copy.10
  83.6 0.8 copy.11

commit v6 on v5

--- a/solution.py
+++ b/solution.py
@@ -386,7 +386,7 @@
         )
 
     def halo_start(img, k, q):
-        last = {0: (0, 1, 2), NQ // 2 - 1: (6, 7), NQ - 1: (8, 9, 3, 4, 5)}
+        last = {0: (0, 1, 2), NQ // 2 - 1: (6, 7), NQ - 1: (4, 5, 3, 8, 9)}
         for n in last.get(q, ()):
 
             @pl.when(exists(pieces[n][:2]))

time: 85.6 us -> 84.8 us (level)
  no operation moved by 1% of the time
where the time goes in v6:
time: 84.8 us; the launch traced here: 83.6 us
  Pallas kernels  81.4 us (96%)
  local copies, waits for them, and re-layouts  1.59 us (2%)
    pallas_call x1, Pallas kernels, per_device(): pl.pallas_call(functools.partial(kernel, rows_axis, cols_axis), out_shape...  81.4 us

profile of v6, /device:TPU:117, one launch (start us, length us, event | category | flops | bytes accessed | tf_op | source)
XLA Modules:
  0.0 83.6 jit_solution(15009071666895942465)
XLA Ops:
  0.6 81.4 %shard_map.77 = (bf16[32,64,128]{2,1,0:T(8,128)(2,1)S(1)}, bf16[32,64,128]{2,1,0:T(8,128)(2,1)S(1)}) custom-call(bf16[32,64,128]{2,1,0:T(8,128)(2,1)} %bitcast.8, bf16[3,3,64,64]{3,2,1,0:T(8,128)(2,1)} %w_first_hbm.1, f32[1,64]{1,0:T(1,128)} %bitcast.10, bf16[3,3,64,64]{3,2,1,0:T(8,128)(2,1)} %w_second_hbm.1, f32[1,64]{1,0:T(1,128)} %bitcast.11, ...), custom_call_target="tpu_custom_call" | custom-call | tf_op jit(solution)/shard_map/pallas_call | solution.py:538
  82.1 0.8 copy.10
  82.9 0.8 copy.11

commit v7 on v6

--- a/solution.py
+++ b/solution.py
@@ -386,7 +386,7 @@
         )
 
     def halo_start(img, k, q):
-        last = {0: (0, 1, 2), NQ // 2 - 1: (6, 7), NQ - 1: (4, 5, 3, 8, 9)}
+        last = {0: (1, 2, 0), NQ // 2 - 1: (6, 7), NQ - 1: (4, 5, 3, 8, 9)}
         for n in last.get(q, ()):
 
             @pl.when(exists(pieces[n][:2]))

time: 84.8 us -> 84.8 us (level)
  no operation moved by 1% of the time
where the time goes in v7:
time: 84.8 us; the launch traced here: 83.8 us
  Pallas kernels  81.5 us (96%)
  local copies, waits for them, and re-layouts  1.59 us (2%)
    pallas_call x1, Pallas kernels, per_device(): pl.pallas_call(functools.partial(kernel, rows_axis, cols_axis), out_shape...  81.5 us

profile of v7, /device:TPU:117, one launch (start us, length us, event | category | flops | bytes accessed | tf_op | source)
XLA Modules:
  0.0 83.8 jit_solution(15250785986621483053)
XLA Ops:
  0.6 81.5 %shard_map.77 = (bf16[32,64,128]{2,1,0:T(8,128)(2,1)S(1)}, bf16[32,64,128]{2,1,0:T(8,128)(2,1)S(1)}) custom-call(bf16[32,64,128]{2,1,0:T(8,128)(2,1)} %bitcast.8, bf16[3,3,64,64]{3,2,1,0:T(8,128)(2,1)} %w_first_hbm.1, f32[1,64]{1,0:T(1,128)} %bitcast.10, bf16[3,3,64,64]{3,2,1,0:T(8,128)(2,1)} %w_second_hbm.1, f32[1,64]{1,0:T(1,128)} %bitcast.11, ...), custom_call_target="tpu_custom_call" | custom-call | tf_op jit(solution)/shard_map/pallas_call | solution.py:538
  82.2 0.8 copy.10
  83.0 0.8 copy.11
